TPU v7x, 512 devices: a whole 4x4x16 slice. The times are simulated.
512 devices in a mesh: grp: 8 (over x, core), own: 64 (over z, y).
Axes of the slice: x: 4, y: 4, z: 16, core: 2. Of those that a mesh axis runs over, the one named last changes fastest.
Arguments:
- left: bfloat16 [32768, 128, 64], P(('grp', 'own')), may hold values from -0.75 to 0.75
- right: bfloat16 [32768, 128, 64], P(('grp', 'own')), may hold values from -0.75 to 0.75
- values: bfloat16 [32768, 128], P(('grp', 'own')), may hold values from -6 to 6
- core: bfloat16 [10240, 64, 64], P(('grp', 'own')), may hold values from -6 to 6
- tile_slice: int32 [32768], P(('grp', 'own')), may hold values from 0 to 10239, as said below
- tile_fill: int32 [32768], P(('grp', 'own')), may hold values from 64 to 128
Outputs:
- new_core: bfloat16 [10240, 64, 64], P(('grp', 'own'))
- new_left: bfloat16 [32768, 128, 64], P(('grp', 'own'))
Inputs may be any that keep to these rules, and one draw needn't show every extreme that they name: `tile_slice`: call j // 20 the block of slice j and its remainder mod 64 its class. Among the tiles of one device at most 2 have slices of one class; in every group of 64 consecutive devices some class gets exactly 2 tiles from every device of the group.
All inputs are finite; a program needn't handle non-finite values.
Results may differ from a plain program's by a relative error of at most 0.0052.
Values may be sent and summed in bfloat16 or wider, within the bound.
No kernel may reach another device: no remote copies, remote signals or barrier semaphores. Data moves between devices by JAX's collectives and lax.ppermute only.
A program may use at most 64 MiB of HBM per device.

v0:
```python
import jax
import jax.numpy as jnp
from jax import lax
from jax.sharding import PartitionSpec as P


def tile_terms(left_tiles, right_tiles, value_tiles, fill_counts, slice_tables):
    tile_rows = left_tiles.shape[1]
    projected = jnp.einsum(
        "sea,sab->seb", left_tiles, slice_tables, preferred_element_type=jnp.float32
    )
    predicted = jnp.sum(projected * right_tiles.astype(jnp.float32), axis=-1)
    live_rows = jnp.arange(tile_rows)[None, :] < fill_counts[:, None]
    residual = jnp.where(live_rows, predicted - value_tiles.astype(jnp.float32), 0.0)
    weighted = (residual[:, :, None] * left_tiles.astype(jnp.float32)).astype(jnp.bfloat16)
    return jnp.einsum("sea,seb->sab", weighted, right_tiles, preferred_element_type=jnp.float32)


def body(left, right, values, core, tile_slice, tile_fill):
    owners = lax.axis_size("own")
    groups = lax.axis_size("grp")
    tile_count, tile_rows, rank_width = left.shape
    per_device = core.shape[0]
    local_count = groups * per_device
    slot_cap = 2 * tile_count // owners
    slot_total = owners * slot_cap
    dev_block = tile_slice // per_device
    target_owner = dev_block % owners
    local_slice = dev_block // owners * per_device + tile_slice % per_device
    positions = jnp.arange(tile_count)
    same_owner = target_owner[:, None] == target_owner[None, :]
    earlier = positions[None, :] < positions[:, None]
    rank_among = jnp.sum((same_owner & earlier).astype(jnp.int32), axis=1)
    slot_of_tile = target_owner * slot_cap + rank_among
    slot_match = slot_of_tile[None, :] == jnp.arange(slot_total)[:, None]
    slot_live = jnp.any(slot_match, axis=1)
    tile_of_slot = jnp.sum(jnp.where(slot_match, positions[None, :], 0), axis=1)
    send_slice = jnp.where(slot_live, local_slice[tile_of_slot], 0)
    old_tables = lax.all_gather(core, "grp", axis=0, tiled=True)
    send_left = left[tile_of_slot]
    send_right = right[tile_of_slot]
    send_values = values[tile_of_slot]
    send_fill = jnp.where(slot_live, tile_fill[tile_of_slot], 0)
    got_left, got_right, got_values, got_slice, got_fill = (
        lax.all_to_all(send_left, "own", split_axis=0, concat_axis=0, tiled=True),
        lax.all_to_all(send_right, "own", split_axis=0, concat_axis=0, tiled=True),
        lax.all_to_all(send_values, "own", split_axis=0, concat_axis=0, tiled=True),
        lax.all_to_all(send_slice, "own", split_axis=0, concat_axis=0, tiled=True),
        lax.all_to_all(send_fill, "own", split_axis=0, concat_axis=0, tiled=True),
    )
    tile_grad = tile_terms(got_left, got_right, got_values, got_fill, old_tables[got_slice])
    selector = (got_slice[:, None] == jnp.arange(local_count)[None, :]).astype(jnp.float32)
    grad_part = jnp.dot(
        selector.T,
        tile_grad.reshape(slot_total, rank_width * rank_width),
        precision=lax.Precision.HIGHEST,
        preferred_element_type=jnp.float32,
    ).reshape(local_count, rank_width, rank_width)
    grad_whole = lax.psum(grad_part, "grp")
    new_tables = (old_tables.astype(jnp.float32) - grad_whole).astype(jnp.bfloat16)
    new_mine = lax.dynamic_slice_in_dim(
        new_tables, lax.axis_index("grp") * per_device, per_device, 0
    )
    refreshed = jnp.einsum(
        "sea,sab->seb", got_left, new_tables[got_slice], preferred_element_type=jnp.float32
    ).astype(jnp.bfloat16)
    returned = lax.all_to_all(refreshed, "own", split_axis=0, concat_axis=0, tiled=True)
    new_left = returned[slot_of_tile]
    return (new_mine, new_left)


def solution(mesh):
    return jax.shard_map(
        body,
        mesh=mesh,
        in_specs=(
            P(("grp", "own"), None, None),
            P(("grp", "own"), None, None),
            P(("grp", "own"), None),
            P(("grp", "own"), None, None),
            P(("grp", "own")),
            P(("grp", "own")),
        ),
        out_specs=(P(("grp", "own"), None, None), P(("grp", "own"), None, None)),
        check_vma=False,
    )
```

profile of v0, /device:TPU:7, one launch (start us, length us, event | category | flops | bytes accessed | tf_op | source)
XLA Modules:
  0.0 528.3 jit_solution(8652673713095691326)
XLA Ops:
  7.2 0.8 fusion.10
  8.0 0.2 convert_reduce_fusion
  8.2 0.1 select_reduce_fusion
  8.2 0.1 fusion.8
  8.4 1.2 gather_fusion
  9.6 1.6 gather_fusion.1
  11.2 0.8 select_n.98
  12.0 18.5 %all-to-all-start.1 = ((s32[64,2,1]{1,2,0:T(1,128)}), s32[64,2,1]{1,2,0:T(1,128)S(1)}, u32[]{:S(2)}, u32[]{:S(2)}) async-start(s32[64,2,1]{1,2,0:T(1,128)} %bitcast.4), calls=%async_computation.1 | async-start | bytes 65536 | tf_op jit(solution)/shard_map/all_to_all | solution.py:49
  30.4 0.8 select_n.96
  31.2 12.7 %all-to-all-done.1 = s32[64,2,1]{1,2,0:T(1,128)S(1)} async-done(((s32[64,2,1]{1,2,0:T(1,128)}), s32[64,2,1]{1,2,0:T(1,128)S(1)}, u32[]{:S(2)}, u32[]{:S(2)}) %all-to-all-start.1) | async-done | bytes 544 | tf_op jit(solution)/shard_map/all_to_all | solution.py:49
  43.8 4.6 all-to-all-start
  48.4 2.1 gather_fusion.4
  50.6 11.4 %all-to-all-done = s32[64,2,1]{1,2,0:T(1,128)S(1)} async-done(((s32[64,2,1]{1,2,0:T(1,128)}), s32[64,2,1]{1,2,0:T(1,128)S(1)}, u32[]{:S(2)}, u32[]{:S(2)}) %all-to-all-start) | async-done | bytes 544 | tf_op jit(solution)/shard_map/all_to_all | solution.py:48
  61.9 4.7 all-to-all-start.3
  66.6 3.4 gather_fusion.2
  70.0 90.1 %all-to-all-done.3 = bf16[128,128,64]{1,2,0:T(8,128)(2,1)S(1)} async-done(((bf16[128,128,64]{1,2,0:T(8,128)(2,1)}), bf16[128,128,64]{1,2,0:T(8,128)(2,1)S(1)}, u32[]{:S(2)}, u32[]{:S(2)}) %all-to-all-start.3) | async-done | bytes 2097184 | tf_op jit(solution)/shard_map/all_to_all | solution.py:46
  160.2 1.3 copy-done.1
  161.5 10.7 %all-to-all-start.2 = ((bf16[128,128,64]{1,2,0:T(8,128)(2,1)}), bf16[128,128,64]{1,2,0:T(8,128)(2,1)S(1)}, u32[]{:S(2)}, u32[]{:S(2)}) async-start(bf16[128,128,64]{1,2,0:T(8,128)(2,1)} %gather_fusion.2), calls=%async_computation.2 | async-start | bytes 4194304 | tf_op jit(solution)/shard_map/all_to_all | solution.py:45
  172.2 0.7 all-gather.2.cloned.1.call-update
  172.9 1.3 gather_fusion.5
  174.3 0.5 broadcast.127
  174.8 0.7 reduce.8
  175.5 0.1 lt.81
  175.6 0.1 all_to_all.28
  175.8 0.7 reduce.9
  176.5 0.1 eq.50
  176.7 34.6 %all-gather.2.cloned.1.call-done = bf16[160,64,64]{2,1,0:T(8,128)(2,1)} async-done(((bf16[20,64,64]{2,1,0:T(8,128)(2,1)}), bf16[160,64,64]{2,1,0:T(8,128)(2,1)}) %all-gather.2.cloned.1.call-update) | async-done | bytes 1310736 | tf_op jit(solution)/shard_map/all_gather | solution.py:39
  211.3 3.9 gather_fusion.3
  215.2 50.7 %all-to-all-done.2 = bf16[128,128,64]{1,2,0:T(8,128)(2,1)S(1)} async-done(((bf16[128,128,64]{1,2,0:T(8,128)(2,1)}), bf16[128,128,64]{1,2,0:T(8,128)(2,1)S(1)}, u32[]{:S(2)}, u32[]{:S(2)}) %all-to-all-start.2) | async-done | bytes 2097184 | tf_op jit(solution)/shard_map/all_to_all | solution.py:45
  265.9 11.0 %all-to-all-start.4 = ((bf16[64,2,128]{2,1,0:T(2,128)(2,1)}), bf16[64,2,128]{2,1,0:T(2,128)(2,1)S(1)}, u32[]{:S(2)}, u32[]{:S(2)}) async-start(bf16[64,2,128]{2,1,0:T(2,128)(2,1)} %bitcast.6), calls=%async_computation.4 | async-start | bytes 65536 | tf_op jit(solution)/shard_map/all_to_all | solution.py:47
  276.9 0.2 all-reduce.2.cloned.1.call-start
  277.1 3.2 multiply_reduce_fusion
  280.4 9.9 %all-to-all-done.4 = bf16[64,2,128]{2,1,0:T(2,128)(2,1)S(1)} async-done(((bf16[64,2,128]{2,1,0:T(2,128)(2,1)}), bf16[64,2,128]{2,1,0:T(2,128)(2,1)S(1)}, u32[]{:S(2)}, u32[]{:S(2)}) %all-to-all-start.4) | async-done | bytes 32800 | tf_op jit(solution)/shard_map/all_to_all | solution.py:47
  290.3 0.1 fusion.6
  290.4 4.8 fusion
  295.2 4.8 copy.30
  299.9 5.4 %fusion.1 = f32[160,64,64]{0,2,1:T(8,128)} fusion(f32[128,64,64]{0,2,1:T(8,128)} %copy.30, s32[128]{0:T(128)S(1)} %eq.50), kind=kOutput, calls=%fused_computation.12 | convolution fusion | flops 1006653440 | bytes 4719104 | tf_op jit(solution)/shard_map/dot_general | solution.py:53
  305.3 4.9 copy.26
  310.3 75.1 %all-reduce.2.cloned.1.call-done = f32[160,64,64]{0,2,1:T(8,128)} async-done(((f32[160,64,64]{0,2,1:T(8,128)}), f32[160,64,64]{0,2,1:T(8,128)}) %all-reduce.2.cloned.1.call-update) | async-done | bytes 2621456 | tf_op jit(solution)/shard_map/psum | solution.py:59
  385.4 5.0 subtract_convert_fusion
  390.4 5.0 copy.31
  395.4 3.9 gather_fusion.6
  399.3 3.8 convolution_convert_fusion
  403.0 15.8 %all-to-all-start.5 = ((bf16[128,128,64]{1,2,0:T(8,128)(2,1)}), bf16[128,128,64]{1,2,0:T(8,128)(2,1)}, u32[]{:S(2)}, u32[]{:S(2)}) async-start(bf16[128,128,64]{1,2,0:T(8,128)(2,1)} %convolution_convert_fusion), calls=%async_computation.5 | async-start | bytes 4194304 | tf_op jit(solution)/shard_map/all_to_all | solution.py:67
  418.8 1.5 constant_dynamic-slice_fusion
  420.3 2.6 copy.33
  422.8 95.4 %all-to-all-done.5 = bf16[128,128,64]{1,2,0:T(8,128)(2,1)} async-done(((bf16[128,128,64]{1,2,0:T(8,128)(2,1)}), bf16[128,128,64]{1,2,0:T(8,128)(2,1)}, u32[]{:S(2)}, u32[]{:S(2)}) %all-to-all-start.5) | async-done | bytes 2097184 | tf_op jit(solution)/shard_map/all_to_all | solution.py:67
  518.3 3.2 gather_fusion.7
  (17 shorter events, 0.1 us)
Async XLA Ops:
  7.2 41.3 %copy-start = (bf16[64,128,64]{1,2,0:T(8,128)(2,1)S(1)}, bf16[64,128,64]{1,2,0:T(8,128)(2,1)}, u32[]{:S(2)}) copy-start(bf16[64,128,64]{1,2,0:T(8,128)(2,1)} %param.7) | copy-start | bytes 3145732
  12.0 31.9 %all-to-all-start.1 = ((s32[64,2,1]{1,2,0:T(1,128)}), s32[64,2,1]{1,2,0:T(1,128)S(1)}, u32[]{:S(2)}, u32[]{:S(2)}) async-start(s32[64,2,1]{1,2,0:T(1,128)} %bitcast.4), calls=%async_computation.1 | async-start | bytes 65536 | tf_op jit(solution)/shard_map/all_to_all | solution.py:49
  43.8 18.1 %all-to-all-start = ((s32[64,2,1]{1,2,0:T(1,128)}), s32[64,2,1]{1,2,0:T(1,128)S(1)}, u32[]{:S(2)}, u32[]{:S(2)}) async-start(s32[64,2,1]{1,2,0:T(1,128)} %bitcast.2), calls=%async_computation | async-start | bytes 65536 | tf_op jit(solution)/shard_map/all_to_all | solution.py:48
  61.9 98.2 %all-to-all-start.3 = ((bf16[128,128,64]{1,2,0:T(8,128)(2,1)}), bf16[128,128,64]{1,2,0:T(8,128)(2,1)S(1)}, u32[]{:S(2)}, u32[]{:S(2)}) async-start(bf16[128,128,64]{1,2,0:T(8,128)(2,1)} %gather_fusion.4), calls=%async_computation.3 | async-start | bytes 4194304 | tf_op jit(solution)/shard_map/all_to_all | solution.py:46
  70.0 102.9 %copy-start.3 = (bf16[64,128]{1,0:T(8,128)(2,1)S(1)}, bf16[64,128]{1,0:T(8,128)(2,1)}, u32[]{:S(2)}) copy-start(bf16[64,128]{1,0:T(8,128)(2,1)} %param.8) | copy-start | bytes 49156
  160.2 1.3 copy-start.1
  161.5 104.4 %all-to-all-start.2 = ((bf16[128,128,64]{1,2,0:T(8,128)(2,1)}), bf16[128,128,64]{1,2,0:T(8,128)(2,1)S(1)}, u32[]{:S(2)}, u32[]{:S(2)}) async-start(bf16[128,128,64]{1,2,0:T(8,128)(2,1)} %gather_fusion.2), calls=%async_computation.2 | async-start | bytes 4194304 | tf_op jit(solution)/shard_map/all_to_all | solution.py:45
  172.2 39.1 %all-gather.2.cloned.1.call-start = ((), (), s32[]{:S(2)}) async-start(), calls=%async_computation.6 | async-start | bytes 2949120 | tf_op jit(solution)/shard_map/all_gather | solution.py:39
  265.9 24.4 %all-to-all-start.4 = ((bf16[64,2,128]{2,1,0:T(2,128)(2,1)}), bf16[64,2,128]{2,1,0:T(2,128)(2,1)S(1)}, u32[]{:S(2)}, u32[]{:S(2)}) async-start(bf16[64,2,128]{2,1,0:T(2,128)(2,1)} %bitcast.6), calls=%async_computation.4 | async-start | bytes 65536 | tf_op jit(solution)/shard_map/all_to_all | solution.py:47
  276.9 108.5 %all-reduce.2.cloned.1.call-start = ((), (), s32[]{:S(2)}) async-start(), calls=%async_computation.7 | async-start | bytes 8388608 | tf_op jit(solution)/shard_map/psum | solution.py:59
  403.0 15.8 %copy-start.2 = (bf16[160,64,64]{0,2,1:T(8,128)(2,1)S(1)}, bf16[160,64,64]{0,2,1:T(8,128)(2,1)}, u32[]{:S(2)}) copy-start(bf16[160,64,64]{0,2,1:T(8,128)(2,1)} %subtract_convert_fusion) | copy-start | bytes 3932164
  403.0 115.2 %all-to-all-start.5 = ((bf16[128,128,64]{1,2,0:T(8,128)(2,1)}), bf16[128,128,64]{1,2,0:T(8,128)(2,1)}, u32[]{:S(2)}, u32[]{:S(2)}) async-start(bf16[128,128,64]{1,2,0:T(8,128)(2,1)} %convolution_convert_fusion), calls=%async_computation.5 | async-start | bytes 4194304 | tf_op jit(solution)/shard_map/all_to_all | solution.py:67
Sparse Core Ops, SparseCore 0:
  175.1 36.1 all-gather.1
  305.5 79.8 all-reduce.1
where the time goes:
time: 529 us; the launch traced here: 528 us
  waiting for transfers between devices  381 us (72%)
  starting transfers between devices  65.5 us (12%)
  local copies, waits for them, and re-layouts  43.1 us (8%)
  matrix products  17.1 us (3%)
  between operations  14.2 us (3%)
  other arithmetic  7.74 us (1%)
    all_to_all x1, waiting for transfers between devices, body(): lax.all_to_all(refreshed, 'own', split_axis=0, concat_axis=0, tiled=True)  95.4 us
    all_to_all x1, waiting for transfers between devices, body(): lax.all_to_all(send_right, 'own', split_axis=0, concat_axis=0, tiled=True)  90.1 us
    psum x1, waiting for transfers between devices, body(): grad_whole = lax.psum(grad_part, 'grp')  75.1 us
    all_to_all x1, waiting for transfers between devices, body(): lax.all_to_all(send_left, 'own', split_axis=0, concat_axis=0, tiled=True)  50.7 us
    all_gather x1, waiting for transfers between devices, body(): old_tables = lax.all_gather(core, 'grp', axis=0, tiled=True)  34.6 us
    all_to_all x1, starting transfers between devices, body(): lax.all_to_all(send_fill, 'own', split_axis=0, concat_axis=0, tiled=True)  18.5 us
    all_to_all x1, starting transfers between devices, body(): lax.all_to_all(refreshed, 'own', split_axis=0, concat_axis=0, tiled=True)  15.8 us
    all_to_all x1, waiting for transfers between devices, body(): lax.all_to_all(send_fill, 'own', split_axis=0, concat_axis=0, tiled=True)  12.7 us
  transfers between devices with their start and end apart: 8, of which 8 were waited for; matrix products, arithmetic and copies ran while one was open for 5% of the time, Pallas kernels for 0%

commit v1 on v0

--- a/solution.py
+++ b/solution.py
@@ -56,7 +56,7 @@
         precision=lax.Precision.HIGHEST,
         preferred_element_type=jnp.float32,
     ).reshape(local_count, rank_width, rank_width)
-    grad_whole = lax.psum(grad_part, "grp")
+    grad_whole = jnp.sum(lax.all_gather(grad_part, "grp"), axis=0)
     new_tables = (old_tables.astype(jnp.float32) - grad_whole).astype(jnp.bfloat16)
     new_mine = lax.dynamic_slice_in_dim(
         new_tables, lax.axis_index("grp") * per_device, per_device, 0

time: 529 us -> 661 us (1.25)
  waiting for transfers between devices: 381 us -> 498 us
  other arithmetic: 7.74 us -> 26.9 us
  local copies, waits for them, and re-layouts: 43.1 us -> 33.1 us
    all_gather x0 -> x1, waiting for transfers between devices: none -> 191 us  [body(): grad_whole = jnp.sum(lax.all_gather(grad_part, 'grp'), axis=0)]
    psum x1 -> x0, waiting for transfers between devices: 75.1 us -> none  [body(): grad_whole = lax.psum(grad_part, 'grp')]
    all_to_all x1, waiting for transfers between devices: 50.7 us -> 91.4 us  [body(): lax.all_to_all(send_left, 'own', split_axis=0, concat_axis=0, tiled=True)]
    all_to_all x1, waiting for transfers between devices: 90.1 us -> 50.6 us  [body(): lax.all_to_all(send_right, 'own', split_axis=0, concat_axis=0, tiled=True)]
    reduce_sum x0 -> x1, other arithmetic: none -> 18.5 us  [body(): grad_whole = jnp.sum(lax.all_gather(grad_part, 'grp'), axis=0)]
    all_to_all x1, starting transfers between devices: 18.5 us -> 4.59 us  [body(): lax.all_to_all(send_fill, 'own', split_axis=0, concat_axis=0, tiled=True)]
    all_to_all x1, starting transfers between devices: 4.59 us -> 18.5 us  [body(): lax.all_to_all(send_slice, 'own', split_axis=0, concat_axis=0, tiled=True)]
  transfers between devices with their start and end apart: 8 -> 8, of which waited for: 8 -> 8; matrix products, arithmetic and copies ran while one was open for 5% -> 3% of each run, Pallas kernels for 0% -> 0%
where the time goes in v1:
time: 661 us; the launch traced here: 654 us
  waiting for transfers between devices  498 us (75%)
  starting transfers between devices  65.3 us (10%)
  local copies, waits for them, and re-layouts  33.1 us (5%)
  other arithmetic  26.9 us (4%)
  matrix products  17.1 us (3%)
  between operations  14.2 us (2%)
    all_gather x1, waiting for transfers between devices, body(): grad_whole = jnp.sum(lax.all_gather(grad_part, 'grp'), axis=0)  191 us
    all_to_all x1, waiting for transfers between devices, body(): lax.all_to_all(refreshed, 'own', split_axis=0, concat_axis=0, tiled=True)  95.2 us
    all_to_all x1, waiting for transfers between devices, body(): lax.all_to_all(send_left, 'own', split_axis=0, concat_axis=0, tiled=True)  91.4 us
    all_to_all x1, waiting for transfers between devices, body(): lax.all_to_all(send_right, 'own', split_axis=0, concat_axis=0, tiled=True)  50.6 us
    all_gather x1, waiting for transfers between devices, body(): old_tables = lax.all_gather(core, 'grp', axis=0, tiled=True)  34.6 us
    reduce_sum x1, other arithmetic, body(): grad_whole = jnp.sum(lax.all_gather(grad_part, 'grp'), axis=0)  18.5 us
    all_to_all x1, starting transfers between devices, body(): lax.all_to_all(send_slice, 'own', split_axis=0, concat_axis=0, tiled=True)  18.5 us
    all_to_all x1, starting transfers between devices, body(): lax.all_to_all(refreshed, 'own', split_axis=0, concat_axis=0, tiled=True)  15.4 us
  transfers between devices with their start and end apart: 8, of which 8 were waited for; matrix products, arithmetic and copies ran while one was open for 3% of the time, Pallas kernels for 0%

profile of v1, /device:TPU:7, one launch (start us, length us, event | category | flops | bytes accessed | tf_op | source)
XLA Modules:
  0.0 654.5 jit_solution(7932996817811939627)
XLA Ops:
  7.2 0.8 fusion.10
  8.0 0.2 convert_reduce_fusion
  8.2 0.1 select_reduce_fusion
  8.2 0.1 fusion.8
  8.4 1.2 gather_fusion
  9.6 1.6 gather_fusion.1
  11.2 0.8 select_n.96
  12.0 18.5 %all-to-all-start = ((s32[64,2,1]{1,2,0:T(1,128)}), s32[64,2,1]{1,2,0:T(1,128)S(1)}, u32[]{:S(2)}, u32[]{:S(2)}) async-start(s32[64,2,1]{1,2,0:T(1,128)} %bitcast.2), calls=%async_computation | async-start | bytes 65536 | tf_op jit(solution)/shard_map/all_to_all | solution.py:48
  30.4 0.8 select_n.98
  31.2 12.7 %all-to-all-done = s32[64,2,1]{1,2,0:T(1,128)S(1)} async-done(((s32[64,2,1]{1,2,0:T(1,128)}), s32[64,2,1]{1,2,0:T(1,128)S(1)}, u32[]{:S(2)}, u32[]{:S(2)}) %all-to-all-start) | async-done | bytes 544 | tf_op jit(solution)/shard_map/all_to_all | solution.py:48
  43.8 4.6 all-to-all-start.1
  48.4 2.1 gather_fusion.2
  50.6 11.4 %all-to-all-done.1 = s32[64,2,1]{1,2,0:T(1,128)S(1)} async-done(((s32[64,2,1]{1,2,0:T(1,128)}), s32[64,2,1]{1,2,0:T(1,128)S(1)}, u32[]{:S(2)}, u32[]{:S(2)}) %all-to-all-start.1) | async-done | bytes 544 | tf_op jit(solution)/shard_map/all_to_all | solution.py:49
  61.9 4.7 all-to-all-start.2
  66.7 2.1 gather_fusion.4
  68.8 91.4 %all-to-all-done.2 = bf16[128,128,64]{1,2,0:T(8,128)(2,1)S(1)} async-done(((bf16[128,128,64]{1,2,0:T(8,128)(2,1)}), bf16[128,128,64]{1,2,0:T(8,128)(2,1)S(1)}, u32[]{:S(2)}, u32[]{:S(2)}) %all-to-all-start.2) | async-done | bytes 2097184 | tf_op jit(solution)/shard_map/all_to_all | solution.py:45
  160.2 11.0 %all-to-all-start.3 = ((bf16[128,128,64]{1,2,0:T(8,128)(2,1)}), bf16[128,128,64]{1,2,0:T(8,128)(2,1)}, u32[]{:S(2)}, u32[]{:S(2)}) async-start(bf16[128,128,64]{1,2,0:T(8,128)(2,1)} %gather_fusion.4), calls=%async_computation.3 | async-start | bytes 4194304 | tf_op jit(solution)/shard_map/all_to_all | solution.py:46
  171.1 0.0 all-gather.4.cloned.1.call-start
  171.2 0.7 all-gather.4.cloned.1.call-update
  171.9 1.3 gather_fusion.5
  173.2 0.1 all_to_all.28
  173.3 0.5 broadcast.127
  173.9 0.7 reduce.8
  174.6 0.1 lt.81
  174.7 0.7 reduce.9
  175.5 0.1 eq.50
  175.6 34.6 %all-gather.4.cloned.1.call-done = bf16[160,64,64]{2,1,0:T(8,128)(2,1)} async-done(((bf16[20,64,64]{2,1,0:T(8,128)(2,1)}), bf16[160,64,64]{2,1,0:T(8,128)(2,1)}) %all-gather.4.cloned.1.call-update) | async-done | bytes 1310736 | tf_op jit(solution)/shard_map/all_gather | solution.py:39
  210.2 3.9 gather_fusion.3
  214.0 50.6 %all-to-all-done.3 = bf16[128,128,64]{1,2,0:T(8,128)(2,1)} async-done(((bf16[128,128,64]{1,2,0:T(8,128)(2,1)}), bf16[128,128,64]{1,2,0:T(8,128)(2,1)}, u32[]{:S(2)}, u32[]{:S(2)}) %all-to-all-start.3) | async-done | bytes 2097184 | tf_op jit(solution)/shard_map/all_to_all | solution.py:46
  264.7 11.0 %all-to-all-start.4 = ((bf16[64,2,128]{2,1,0:T(2,128)(2,1)}), bf16[64,2,128]{2,1,0:T(2,128)(2,1)S(1)}, u32[]{:S(2)}, u32[]{:S(2)}) async-start(bf16[64,2,128]{2,1,0:T(2,128)(2,1)} %bitcast.6), calls=%async_computation.4 | async-start | bytes 65536 | tf_op jit(solution)/shard_map/all_to_all | solution.py:47
  275.7 0.2 all-gather.6.cloned.1.call-start
  275.9 3.2 multiply_reduce_fusion
  279.2 9.9 %all-to-all-done.4 = bf16[64,2,128]{2,1,0:T(2,128)(2,1)S(1)} async-done(((bf16[64,2,128]{2,1,0:T(2,128)(2,1)}), bf16[64,2,128]{2,1,0:T(2,128)(2,1)S(1)}, u32[]{:S(2)}, u32[]{:S(2)}) %all-to-all-start.4) | async-done | bytes 32800 | tf_op jit(solution)/shard_map/all_to_all | solution.py:47
  289.1 0.1 fusion.6
  289.2 4.8 fusion
  293.9 4.8 copy.32
  298.7 5.3 fusion.1
  304.1 6.2 copy.33
  310.3 0.0 all-gather.6.cloned.1.call-update
  310.3 191.3 %all-gather.6.cloned.1.call-done = f32[1280,64,64]{2,1,0:T(8,128)} async-done(((f32[160,64,64]{2,1,0:T(8,128)}), f32[1280,64,64]{2,1,0:T(8,128)}) %all-gather.6.cloned.1.call-update) | async-done | bytes 20971536 | tf_op jit(solution)/shard_map/all_gather | solution.py:59
  501.6 18.5 %reduce_sum.42 = f32[160,64,64]{2,1,0:T(8,128)} reduce(f32[8,160,64,64]{3,2,1,0:T(8,128)} %bitcast.30, f32[]{:T(128)} %constant.58.clone.1), dimensions={0}, to_apply=%region_4.5 | reduce | flops 4587520 | bytes 23592964 | tf_op jit(solution)/shard_map/reduce_sum | solution.py:59
  520.2 5.7 subtract_convert_fusion
  525.9 3.9 gather_fusion.6
  529.8 3.8 convolution_convert_fusion
  533.6 15.4 %all-to-all-start.5 = ((bf16[128,128,64]{1,2,0:T(8,128)(2,1)}), bf16[128,128,64]{1,2,0:T(8,128)(2,1)S(1)}, u32[]{:S(2)}, u32[]{:S(2)}) async-start(bf16[128,128,64]{1,2,0:T(8,128)(2,1)} %convolution_convert_fusion), calls=%async_computation.5 | async-start | bytes 4194304 | tf_op jit(solution)/shard_map/all_to_all | solution.py:67
  549.0 1.8 constant_dynamic-slice_fusion
  550.8 95.2 %all-to-all-done.5 = bf16[128,128,64]{1,2,0:T(8,128)(2,1)S(1)} async-done(((bf16[128,128,64]{1,2,0:T(8,128)(2,1)}), bf16[128,128,64]{1,2,0:T(8,128)(2,1)S(1)}, u32[]{:S(2)}, u32[]{:S(2)}) %all-to-all-start.5) | async-done | bytes 2097184 | tf_op jit(solution)/shard_map/all_to_all | solution.py:67
  646.0 1.6 gather_fusion.7
  (16 shorter events, 0.1 us)
Async XLA Ops:
  7.2 41.3 %copy-start = (bf16[64,128,64]{1,2,0:T(8,128)(2,1)S(1)}, bf16[64,128,64]{1,2,0:T(8,128)(2,1)}, u32[]{:S(2)}) copy-start(bf16[64,128,64]{1,2,0:T(8,128)(2,1)} %param.6) | copy-start | bytes 3145732
  12.0 31.9 %all-to-all-start = ((s32[64,2,1]{1,2,0:T(1,128)}), s32[64,2,1]{1,2,0:T(1,128)S(1)}, u32[]{:S(2)}, u32[]{:S(2)}) async-start(s32[64,2,1]{1,2,0:T(1,128)} %bitcast.2), calls=%async_computation | async-start | bytes 65536 | tf_op jit(solution)/shard_map/all_to_all | solution.py:48
  43.8 18.1 %all-to-all-start.1 = ((s32[64,2,1]{1,2,0:T(1,128)}), s32[64,2,1]{1,2,0:T(1,128)S(1)}, u32[]{:S(2)}, u32[]{:S(2)}) async-start(s32[64,2,1]{1,2,0:T(1,128)} %bitcast.4), calls=%async_computation.1 | async-start | bytes 65536 | tf_op jit(solution)/shard_map/all_to_all | solution.py:49
  50.6 16.1 %copy-start.2 = (bf16[64,128,64]{1,2,0:T(8,128)(2,1)S(1)}, bf16[64,128,64]{1,2,0:T(8,128)(2,1)}, u32[]{:S(2)}) copy-start(bf16[64,128,64]{1,2,0:T(8,128)(2,1)} %param.7) | copy-start | bytes 3145732
  61.9 98.2 %all-to-all-start.2 = ((bf16[128,128,64]{1,2,0:T(8,128)(2,1)}), bf16[128,128,64]{1,2,0:T(8,128)(2,1)S(1)}, u32[]{:S(2)}, u32[]{:S(2)}) async-start(bf16[128,128,64]{1,2,0:T(8,128)(2,1)} %gather_fusion.2), calls=%async_computation.2 | async-start | bytes 4194304 | tf_op jit(solution)/shard_map/all_to_all | solution.py:45
  68.8 103.1 %copy-start.3 = (bf16[64,128]{1,0:T(8,128)(2,1)S(1)}, bf16[64,128]{1,0:T(8,128)(2,1)}, u32[]{:S(2)}) copy-start(bf16[64,128]{1,0:T(8,128)(2,1)} %param.8) | copy-start | bytes 49156
  160.2 104.5 %all-to-all-start.3 = ((bf16[128,128,64]{1,2,0:T(8,128)(2,1)}), bf16[128,128,64]{1,2,0:T(8,128)(2,1)}, u32[]{:S(2)}, u32[]{:S(2)}) async-start(bf16[128,128,64]{1,2,0:T(8,128)(2,1)} %gather_fusion.4), calls=%async_computation.3 | async-start | bytes 4194304 | tf_op jit(solution)/shard_map/all_to_all | solution.py:46
  171.1 39.0 %all-gather.4.cloned.1.call-start = ((), (), s32[]{:S(2)}) async-start(), calls=%async_computation.6 | async-start | bytes 2949120 | tf_op jit(solution)/shard_map/all_gather | solution.py:39
  264.7 24.4 %all-to-all-start.4 = ((bf16[64,2,128]{2,1,0:T(2,128)(2,1)}), bf16[64,2,128]{2,1,0:T(2,128)(2,1)S(1)}, u32[]{:S(2)}, u32[]{:S(2)}) async-start(bf16[64,2,128]{2,1,0:T(2,128)(2,1)} %bitcast.6), calls=%async_computation.4 | async-start | bytes 65536 | tf_op jit(solution)/shard_map/all_to_all | solution.py:47
  275.7 225.9 %all-gather.6.cloned.1.call-start = ((), (), s32[]{:S(2)}) async-start(), calls=%async_computation.7 | async-start | bytes 47185920 | tf_op jit(solution)/shard_map/all_gather | solution.py:59
  533.6 112.4 %all-to-all-start.5 = ((bf16[128,128,64]{1,2,0:T(8,128)(2,1)}), bf16[128,128,64]{1,2,0:T(8,128)(2,1)S(1)}, u32[]{:S(2)}, u32[]{:S(2)}) async-start(bf16[128,128,64]{1,2,0:T(8,128)(2,1)} %convolution_convert_fusion), calls=%async_computation.5 | async-start | bytes 4194304 | tf_op jit(solution)/shard_map/all_to_all | solution.py:67
  549.0 98.7 %copy-start.1 = (bf16[64,128,64]{1,2,0:T(8,128)(2,1)S(1)}, bf16[64,128,64]{1,2,0:T(8,128)(2,1)}, u32[]{:S(2)}) copy-start(bf16[64,128,64]{1,2,0:T(8,128)(2,1)} %param.6) | copy-start | bytes 3145732
Sparse Core Ops, SparseCore 0:
  174.1 36.0 all-gather.3
  310.4 191.1 all-gather.5
